TPU v7x, 32 devices: a whole 2x2x4 slice. The times are simulated.
32 devices in a mesh: grp: 1, fsdp: 32 (over z, y, x, core), rep: 1.
Axes of the slice: x: 2, y: 2, z: 4, core: 2. Of those that a mesh axis runs over, the one named last changes fastest.
Arguments:
- items: bfloat16 [1, 16384, 512], P('rep', ('grp', 'fsdp')), may hold values from -30 to 30, as said below
- w_in: bfloat16 [512, 2048], P('fsdp'), may hold values from -0.25 to 0.25
- w_out: bfloat16 [2048, 1024], P('fsdp'), may hold values from -0.125 to 0.125
- users: bfloat16 [1, 1024, 1024], P('rep', ('grp', 'fsdp')), may hold values from -0.19921875 to 0.19921875
- res_codes: int32 [1, 16384, 1024], P('rep', ('grp', 'fsdp')), may hold values from 0 to 15
- range_idx: int32 [1024], P('grp'), may hold values from 0 to 3
- range_lo: float32 [4], P('grp'), may hold values from -1 to 1
- range_step: float32 [4], P('grp'), may hold values from 0.05 to 0.2
Outputs:
- new_codes: bfloat16 [1, 16384, 1024], P('rep', ('grp', 'fsdp'))
- best: float32 [1, 1024], P('rep', ('grp', 'fsdp'))
Inputs may be any that keep to these rules, and one draw needn't show every extreme that they name: `items`: item features of order one.
All inputs are finite; a program needn't handle non-finite values.
Results may differ from a plain program's by a relative error of at most 0.0075.
Values may be sent and summed in bfloat16 or wider, within the bound.
No kernel may reach another device: no remote copies, remote signals or barrier semaphores. Data moves between devices by JAX's collectives and lax.ppermute only.
A program may use at most 64 MiB of HBM per device.

v0:
```python
import jax
import jax.numpy as jnp
from jax import lax
from jax.sharding import PartitionSpec as P


def row_adder(left, piece):
    return jnp.dot(left, piece, preferred_element_type=jnp.float32)


def on_device(items, w_in, w_out, users, res_codes, range_idx, range_lo, range_step):
    features = items[0]
    first = row_adder(features, lax.all_gather(w_in, "fsdp", axis=0, tiled=True))
    hidden = jax.nn.silu(first).astype(jnp.bfloat16)
    embed = row_adder(hidden, lax.all_gather(w_out, "fsdp", axis=0, tiled=True))
    local_upper = jnp.max(embed, axis=0)
    local_lower = jnp.min(embed, axis=0)
    upper = lax.pmax(local_upper, ("fsdp", "rep"))
    lower = lax.pmin(local_lower, ("fsdp", "rep"))
    mid = (upper + lower) * 0.5
    half = (upper - lower) * 0.5
    new_codes = (7.5 * (embed - mid) / (half + 1e-05)).astype(jnp.bfloat16)[None]
    levels = jnp.arange(range_lo.shape[0], dtype=jnp.int32)
    match = (range_idx[None, :] == levels[:, None]).astype(jnp.float32)
    step_d = jnp.sum(range_step[:, None] * match, axis=0)
    lo_d = jnp.sum(range_lo[:, None] * match, axis=0)
    resident = res_codes[0].astype(jnp.bfloat16)
    member = lax.all_gather(users, "fsdp", axis=1, tiled=True)[0]
    folded = (member.astype(jnp.float32) * step_d).astype(jnp.bfloat16)
    offset = jnp.dot(member.astype(jnp.float32), lo_d, precision=lax.Precision.HIGHEST)
    scores = lax.dot_general(
        resident, folded, (((1,), (1,)), ((), ())), preferred_element_type=jnp.float32
    )
    local_best = (jnp.max(scores, axis=0) + offset)[None]
    merged = lax.pmax(local_best, "fsdp")
    count = users.shape[1]
    best = lax.dynamic_slice_in_dim(merged, lax.axis_index("fsdp") * count, count, 1)
    return (new_codes, best)


def solution(mesh):
    return jax.shard_map(
        on_device,
        mesh=mesh,
        in_specs=(
            P("rep", ("grp", "fsdp"), None),
            P("fsdp", None),
            P("fsdp", None),
            P("rep", ("grp", "fsdp"), None),
            P("rep", ("grp", "fsdp"), None),
            P("grp"),
            P("grp"),
            P("grp"),
        ),
        out_specs=(P("rep", ("grp", "fsdp"), None), P("rep", ("grp", "fsdp"))),
        check_vma=False,
    )
```

profile of v0, /device:TPU:0, one launch (start us, length us, event | category | flops | bytes accessed | tf_op | source)
XLA Modules:
  0.0 286.0 jit_solution(5587563280381236445)
XLA Ops:
  7.2 0.0 copy-start
  7.2 0.0 all-gather.8.cloned.1.call-start
  7.2 0.7 all-gather.8.cloned.1.call-update
  7.9 0.0 all-gather.4.cloned.1.call-start
  8.0 0.7 all-gather.4.cloned.1.call-update
  8.7 0.0 all-gather.6.cloned.1.call-start
  8.7 0.7 all-gather.6.cloned.1.call-update
  9.4 0.8 select_reduce_fusion
  10.2 59.8 %all-gather.8.cloned.1.call-done = bf16[1,1024,1024]{2,1,0:T(8,128)(2,1)} async-done(((bf16[1,32,1024]{2,1,0:T(8,128)(2,1)}), bf16[1,1024,1024]{2,1,0:T(8,128)(2,1)}) %all-gather.8.cloned.1.call-update) | async-done | bytes 2097168 | tf_op jit(solution)/shard_map/all_gather | solution.py:28
  70.0 0.0 copy-start.1
  70.0 3.5 %fusion.3 = f32[1,1024]{1,0:T(1,128)S(1)} fusion(f32[1024,1]{0,1:T(1,128)S(1)} %bitcast.29, bf16[1,1024,1024]{2,1,0:T(8,128)(2,1)} %all-gather.8.cloned.1.call-done), kind=kOutput, calls=%fused_computation.4 | convolution fusion | flops 12582912 | bytes 2105344 | tf_op jit(solution)/shard_map/dot_general | solution.py:30
  73.4 0.0 copy-done.1
  73.4 2.9 %fusion.7 = f32[1024]{0:T(1024)S(1)} fusion(bf16[1,1024,1024]{2,1,0:T(8,128)(2,1)S(1)} %copy-done.1, f32[1024]{0:T(1024)S(1)} %get-tuple-element.5, s32[1,512,1024]{2,1,0:T(8,128)} %param.12), kind=kOutput, calls=%fused_computation.9 | convolution fusion | flops 1077935104 | bytes 4202496 | tf_op jit(solution)/shard_map/dot_general | solution.py:31
  76.4 51.7 %all-gather.4.cloned.1.call-done = bf16[512,2048]{1,0:T(8,128)(2,1)} async-done(((bf16[16,2048]{1,0:T(8,128)(2,1)}), bf16[512,2048]{1,0:T(8,128)(2,1)}) %all-gather.4.cloned.1.call-update) | async-done | bytes 2097168 | tf_op jit(solution)/shard_map/all_gather | solution.py:13
  128.1 63.8 %all-gather.6.cloned.1.call-done = bf16[2048,1024]{1,0:T(8,128)(2,1)} async-done(((bf16[64,1024]{1,0:T(8,128)(2,1)}), bf16[2048,1024]{1,0:T(8,128)(2,1)}) %all-gather.6.cloned.1.call-update) | async-done | bytes 4194320 | tf_op jit(solution)/shard_map/all_gather | solution.py:15
  191.9 0.0 copy-done
  191.9 6.4 %fusion.20 = (f32[1024]{0:T(1024)S(1)}, f32[1024]{0:T(1024)S(1)}, f32[512,1024]{1,0:T(8,128)S(1)}) fusion(bf16[2048,1024]{1,0:T(8,128)(2,1)} %all-gather.6.cloned.1.call-done, bf16[512,2048]{1,0:T(8,128)(2,1)} %all-gather.4.cloned.1.call-done, bf16[1,512,512]{2,1,0:T(8,128)(2,1)S(1)} %copy-done), kind=kOutput, calls=%fused_computation.22 | convolution fusion | flops 3227514880 | bytes 8921088 | tf_op jit(solution)/shard_map/dot_general | solution.py:8
  198.3 39.2 %pmin.7 = f32[1024]{0:T(1024)S(1)} all-reduce(f32[1024]{0:T(1024)S(1)} %get-tuple-element.2), channel_id=1, replica_groups=mesh['grp'=1,'fsdp'=32,'rep'=1] {'fsdp','rep'}, use_global_device_ids=true, to_apply=%region_3.4 | all-reduce | flops 1024 | bytes 8192 | tf_op jit(solution)/shard_map/pmin | solution.py:19
  237.5 40.1 %all-reduce = (f32[1024]{0:T(1024)S(1)}, f32[1,1024]{1,0:T(1,128)S(1)}) all-reduce(f32[1024]{0:T(1024)S(1)} %get-tuple-element.3, f32[1,1024]{1,0:T(1,128)S(1)} %bitcast.30), channel_id=1, replica_groups=mesh['grp'=1,'fsdp'=32,'rep'=1] {'fsdp','rep'}, use_global_device_ids=true, to_apply=%region_1.2 | all-reduce | flops 2048 | bytes 16384 | tf_op jit(solution)/shard_map/pmax | solution.py:18
  277.6 0.6 constant_dynamic-slice_fusion
  278.2 1.3 fusion.12
  (2 shorter events, 0.0 us)
Async XLA Ops:
  7.2 184.7 %copy-start = (bf16[1,512,512]{2,1,0:T(8,128)(2,1)S(1)}, bf16[1,512,512]{2,1,0:T(8,128)(2,1)}, u32[]{:S(2)}) copy-start(bf16[1,512,512]{2,1,0:T(8,128)(2,1)} %param.8) | copy-start | bytes 1572868
  7.2 62.8 %all-gather.8.cloned.1.call-start = ((), (), s32[]{:S(2)}) async-start(), calls=%async_computation.2 | async-start | bytes 2162688 | tf_op jit(solution)/shard_map/all_gather | solution.py:28
  7.9 120.2 %all-gather.4.cloned.1.call-start = ((), (), s32[]{:S(2)}) async-start(), calls=%async_computation | async-start | bytes 2162688 | tf_op jit(solution)/shard_map/all_gather | solution.py:13
  8.7 183.2 %all-gather.6.cloned.1.call-start = ((), (), s32[]{:S(2)}) async-start(), calls=%async_computation.1 | async-start | bytes 4325376 | tf_op jit(solution)/shard_map/all_gather | solution.py:15
  70.0 3.5 %copy-start.1 = (bf16[1,1024,1024]{2,1,0:T(8,128)(2,1)S(1)}, bf16[1,1024,1024]{2,1,0:T(8,128)(2,1)}, u32[]{:S(2)}) copy-start(bf16[1,1024,1024]{2,1,0:T(8,128)(2,1)} %all-gather.8.cloned.1.call-done) | copy-start | bytes 6291460
Sparse Core Ops, SparseCore 0:
  10.9 59.0 all-gather.7
  72.8 55.2 all-gather.3
  131.0 60.8 all-gather.5
where the time goes:
time: 286 us
  waiting for transfers between devices  177 us (62%)
  blocking collectives  79.3 us (28%)
  between operations  13.8 us (5%)
  matrix products  12.8 us (4%)
    all_gather x1, waiting for transfers between devices, on_device(): embed = row_adder(hidden, lax.all_gather(w_out, 'fsdp', axis=0, tiled=True))  63.8 us
    all_gather x1, waiting for transfers between devices, on_device(): member = lax.all_gather(users, 'fsdp', axis=1, tiled=True)[0]  59.8 us
    all_gather x1, waiting for transfers between devices, on_device(): lax.all_gather(w_in, 'fsdp', axis=0, tiled=True)  51.7 us
    pmax x1, blocking collectives, on_device(): upper = lax.pmax(local_upper, ('fsdp', 'rep'))  40.1 us
    pmin x1, blocking collectives, on_device(): lower = lax.pmin(local_lower, ('fsdp', 'rep'))  39.2 us
    dot_general x1, matrix products, row_adder(): return jnp.dot(left, piece, preferred_element_type=jnp.float32)  6.45 us
  transfers between devices with their start and end apart: 3, of which 3 were waited for; matrix products, arithmetic and copies ran while one was open for 3% of the time, Pallas kernels for 0%

commit v1 on v0

--- a/solution.py
+++ b/solution.py
@@ -1,7 +1,23 @@
+import functools
 import jax
 import jax.numpy as jnp
 from jax import lax
 from jax.sharding import PartitionSpec as P
+
+
+def make_side_here(x_part, which_dim):
+    reached, answer = (lax.axis_size("fsdp"), lax.axis_index("fsdp"))
+    heard, val = (x_part, 1)
+    while val < reached:
+        local_next = lax.ppermute(heard, "fsdp", list(map(lambda u: (u, u ^ val), range(reached))))
+        side_arr = jnp.concatenate([heard, local_next], axis=which_dim)
+        new = jnp.concatenate([local_next, heard], axis=which_dim)
+        heard = jnp.where(answer & val == 0, side_arr, new)
+        val = 2 * val
+    return heard
+
+
+divide_series_all = functools.partial(make_side_here, which_dim=0)
 
 
 def row_adder(left, piece):
@@ -10,7 +26,7 @@
 
 def on_device(items, w_in, w_out, users, res_codes, range_idx, range_lo, range_step):
     features = items[0]
-    first = row_adder(features, lax.all_gather(w_in, "fsdp", axis=0, tiled=True))
+    first = row_adder(features, divide_series_all(w_in))
     hidden = jax.nn.silu(first).astype(jnp.bfloat16)
     embed = row_adder(hidden, lax.all_gather(w_out, "fsdp", axis=0, tiled=True))
     local_upper = jnp.max(embed, axis=0)

time: 286 us -> 256 us (0.90)
  waiting for transfers between devices: 177 us -> 134 us
  starting transfers between devices: 0.11 us -> 9.25 us
    all_gather x1 -> x0, waiting for transfers between devices: 51.7 us -> none  [on_device(): lax.all_gather(w_in, 'fsdp', axis=0, tiled=True)]
    ppermute x0 -> x5, waiting for transfers between devices: none -> 23 us  [make_side_here(): lax.ppermute(heard, 'fsdp', list(map(lambda u: (u, u ^ val), range(reache...]
    all_gather x1, waiting for transfers between devices: 59.8 us -> 50.5 us  [on_device(): member = lax.all_gather(users, 'fsdp', axis=1, tiled=True)[0]]
    ppermute x0 -> x5, starting transfers between devices: none -> 9.18 us  [make_side_here(): lax.ppermute(heard, 'fsdp', list(map(lambda u: (u, u ^ val), range(reache...]
    all_gather x1, waiting for transfers between devices: 63.8 us -> 59.4 us  [on_device(): embed = row_adder(hidden, lax.all_gather(w_out, 'fsdp', axis=0, tiled=True))]
  transfers between devices with their start and end apart: 3 -> 7, of which waited for: 3 -> 6; matrix products, arithmetic and copies ran while one was open for 3% -> 3% of each run, Pallas kernels for 0% -> 0%
where the time goes in v1:
time: 256 us; the launch traced here: 255 us
  waiting for transfers between devices  134 us (52%)
  blocking collectives  79.3 us (31%)
  between operations  14.2 us (6%)
  matrix products  14 us (5%)
  starting transfers between devices  9.25 us (4%)
  other arithmetic  2.73 us (1%)
    all_gather x1, waiting for transfers between devices, on_device(): embed = row_adder(hidden, lax.all_gather(w_out, 'fsdp', axis=0, tiled=True))  59.4 us
    all_gather x1, waiting for transfers between devices, on_device(): member = lax.all_gather(users, 'fsdp', axis=1, tiled=True)[0]  50.5 us
    pmax x1, blocking collectives, on_device(): upper = lax.pmax(local_upper, ('fsdp', 'rep'))  40.1 us
    pmin x1, blocking collectives, on_device(): lower = lax.pmin(local_lower, ('fsdp', 'rep'))  39.2 us
    ppermute x5, waiting for transfers between devices, make_side_here(): lax.ppermute(heard, 'fsdp', list(map(lambda u: (u, u ^ val), range(reache...  23 us
    ppermute x5, starting transfers between devices, make_side_here(): lax.ppermute(heard, 'fsdp', list(map(lambda u: (u, u ^ val), range(reache...  9.18 us
    dot_general x1, matrix products, row_adder(): return jnp.dot(left, piece, preferred_element_type=jnp.float32)  7.63 us
  transfers between devices with their start and end apart: 7, of which 6 were waited for; matrix products, arithmetic and copies ran while one was open for 3% of the time, Pallas kernels for 0%

profile of v1, /device:TPU:0, one launch (start us, length us, event | category | flops | bytes accessed | tf_op | source)
XLA Modules:
  0.0 255.3 jit_solution(6096046822005243642)
XLA Ops:
  7.3 0.7 all-gather.5.cloned.1.call-update
  8.0 0.7 all-gather.3.cloned.1.call-update
  8.7 0.5 collective-permute-start
  9.2 1.1 collective-permute-done
  10.3 0.9 maximum_select_fusion.9
  11.3 2.9 %collective-permute-start.1 = (bf16[32,2048]{1,0:T(8,128)(2,1)S(1)}, bf16[32,2048]{1,0:T(8,128)(2,1)S(1)}, u32[]{:S(2)}, u32[]{:S(2)}) collective-permute-start(bf16[32,2048]{1,0:T(8,128)(2,1)S(1)} %maximum_select_fusion.9), channel_id=1, source_target_pairs={{0,2},{1,3},{2,0},{3,1},{4,6},{5,7},{6,4},{7,5},{8,10},{9,11},{10,... | collective-permute-start | bytes 393224 | tf_op jit(solution)/shard_map/ppermute | solution.py:12
  14.2 3.8 %collective-permute-done.1 = bf16[32,2048]{1,0:T(8,128)(2,1)S(1)} collective-permute-done((bf16[32,2048]{1,0:T(8,128)(2,1)S(1)}, bf16[32,2048]{1,0:T(8,128)(2,1)S(1)}, u32[]{:S(2)}, u32[]{:S(2)}) %collective-permute-start.1) | collective-permute-done | bytes 131104 | tf_op jit(solution)/shard_map/ppermute | solution.py:12
  18.1 1.8 collective-permute-start.2
  19.9 6.5 %collective-permute-done.2 = bf16[64,2048]{1,0:T(8,128)(2,1)S(1)} collective-permute-done((bf16[64,2048]{1,0:T(8,128)(2,1)S(1)}, bf16[64,2048]{1,0:T(8,128)(2,1)S(1)}, u32[]{:S(2)}, u32[]{:S(2)}) %collective-permute-start.2) | collective-permute-done | bytes 262176 | tf_op jit(solution)/shard_map/ppermute | solution.py:12
  26.4 0.1 maximum_select_fusion.7
  26.5 1.6 collective-permute-start.3
  28.1 11.5 %collective-permute-done.3 = bf16[128,2048]{1,0:T(8,128)(2,1)S(1)} collective-permute-done((bf16[128,2048]{1,0:T(8,128)(2,1)S(1)}, bf16[128,2048]{1,0:T(8,128)(2,1)S(1)}, u32[]{:S(2)}, u32[]{:S(2)}) %collective-permute-start.3) | collective-permute-done | bytes 524320 | tf_op jit(solution)/shard_map/ppermute | solution.py:12
  39.6 0.3 maximum_select_fusion.6
  39.9 2.4 collective-permute-start.4
  42.4 50.5 %all-gather.5.cloned.1.call-done = bf16[1,1024,1024]{2,1,0:T(8,128)(2,1)} async-done(((bf16[1,32,1024]{2,1,0:T(8,128)(2,1)}), bf16[1,1024,1024]{2,1,0:T(8,128)(2,1)}) %all-gather.5.cloned.1.call-update) | async-done | bytes 2097168 | tf_op jit(solution)/shard_map/all_gather | solution.py:44
  92.9 3.5 %fusion.13 = f32[1,1024]{1,0:T(1,128)S(1)} fusion(f32[1024,1]{0,1:T(1,128)S(1)} %bitcast.41, bf16[1,1024,1024]{2,1,0:T(8,128)(2,1)} %all-gather.5.cloned.1.call-done), kind=kOutput, calls=%fused_computation.16 | convolution fusion | flops 12582912 | bytes 2105344 | tf_op jit(solution)/shard_map/dot_general | solution.py:46
  96.3 2.9 %fusion.19 = f32[1024]{0:T(1024)S(1)} fusion(bf16[1,1024,1024]{2,1,0:T(8,128)(2,1)S(1)} %copy-done.1, f32[1024]{0:T(1024)S(1)} %get-tuple-element.5, s32[1,512,1024]{2,1,0:T(8,128)} %param.12), kind=kOutput, calls=%fused_computation.22 | convolution fusion | flops 1077935104 | bytes 4202496 | tf_op jit(solution)/shard_map/dot_general | solution.py:47
  99.3 1.0 copy-done.6
  100.3 59.4 %all-gather.3.cloned.1.call-done = bf16[2048,1024]{1,0:T(8,128)(2,1)} async-done(((bf16[64,1024]{1,0:T(8,128)(2,1)}), bf16[2048,1024]{1,0:T(8,128)(2,1)}) %all-gather.3.cloned.1.call-update) | async-done | bytes 4194320 | tf_op jit(solution)/shard_map/all_gather | solution.py:31
  159.7 7.6 %fusion.30 = (f32[1024]{0:T(1024)S(1)}, f32[1024]{0:T(1024)S(1)}, f32[512,1024]{1,0:T(8,128)S(1)}) fusion(bf16[2048,1024]{1,0:T(8,128)(2,1)} %all-gather.3.cloned.1.call-done, bf16[256,2048]{1,0:T(8,128)(2,1)} %copy-done.6, bf16[256,2048]{1,0:T(8,128)(2,1)} %copy-done.2, pred[]{:T(512)S(6)} %eq.28, bf16[1,512,512]{2,1,0:T(8,128)(2,1)S(1)} %copy-done), kind=kOutput, calls=%fused_computation.39 | convolution fusion | flops 3236952064 | bytes 8921089 | tf_op jit(solution)/shard_map/dot_general | solution.py:24
  167.3 39.2 %pmin.7 = f32[1024]{0:T(1024)S(1)} all-reduce(f32[1024]{0:T(1024)S(1)} %get-tuple-element.2), channel_id=1, replica_groups=mesh['grp'=1,'fsdp'=32,'rep'=1] {'fsdp','rep'}, use_global_device_ids=true, to_apply=%region_3.4 | all-reduce | flops 1024 | bytes 8192 | tf_op jit(solution)/shard_map/pmin | solution.py:35
  206.5 40.1 %all-reduce = (f32[1024]{0:T(1024)S(1)}, f32[1,1024]{1,0:T(1,128)S(1)}) all-reduce(f32[1024]{0:T(1024)S(1)} %get-tuple-element.3, f32[1,1024]{1,0:T(1,128)S(1)} %bitcast.42), channel_id=1, replica_groups=mesh['grp'=1,'fsdp'=32,'rep'=1] {'fsdp','rep'}, use_global_device_ids=true, to_apply=%region_1.2 | all-reduce | flops 2048 | bytes 16384 | tf_op jit(solution)/shard_map/pmax | solution.py:34
  246.6 0.6 constant_dynamic-slice_fusion
  247.2 1.3 fusion.24
  (20 shorter events, 0.3 us)
Async XLA Ops:
  7.2 152.5 %copy-start = (bf16[1,512,512]{2,1,0:T(8,128)(2,1)S(1)}, bf16[1,512,512]{2,1,0:T(8,128)(2,1)}, u32[]{:S(2)}) copy-start(bf16[1,512,512]{2,1,0:T(8,128)(2,1)} %param.8) | copy-start | bytes 1572868
  7.2 35.1 %copy-start.3 = (s32[1024]{0:T(1024)S(1)}, s32[1024]{0:T(1024)}, u32[]{:S(2)}) copy-start(s32[1024]{0:T(1024)} %param.13) | copy-start | bytes 12292
  7.2 35.1 %copy-start.4 = (f32[4]{0:T(128)S(1)}, f32[4]{0:T(128)}, u32[]{:S(2)}) copy-start(f32[4]{0:T(128)} %param.14) | copy-start | bytes 52
  7.2 35.1 %copy-start.5 = (f32[4]{0:T(128)S(1)}, f32[4]{0:T(128)}, u32[]{:S(2)}) copy-start(f32[4]{0:T(128)} %param.15) | copy-start | bytes 52
  7.2 85.7 %all-gather.5.cloned.1.call-start = ((), (), s32[]{:S(2)}) async-start(), calls=%async_computation.1 | async-start | bytes 2162688 | tf_op jit(solution)/shard_map/all_gather | solution.py:44
  7.9 151.7 %all-gather.3.cloned.1.call-start = ((), (), s32[]{:S(2)}) async-start(), calls=%async_computation | async-start | bytes 4325376 | tf_op jit(solution)/shard_map/all_gather | solution.py:31
  8.7 1.6 collective-permute-start
  11.3 6.7 %collective-permute-start.1 = (bf16[32,2048]{1,0:T(8,128)(2,1)S(1)}, bf16[32,2048]{1,0:T(8,128)(2,1)S(1)}, u32[]{:S(2)}, u32[]{:S(2)}) collective-permute-start(bf16[32,2048]{1,0:T(8,128)(2,1)S(1)} %maximum_select_fusion.9), channel_id=1, source_target_pairs={{0,2},{1,3},{2,0},{3,1},{4,6},{5,7},{6,4},{7,5},{8,10},{9,11},{10,... | collective-permute-start | bytes 393224 | tf_op jit(solution)/shard_map/ppermute | solution.py:12
  18.1 8.4 %collective-permute-start.2 = (bf16[64,2048]{1,0:T(8,128)(2,1)S(1)}, bf16[64,2048]{1,0:T(8,128)(2,1)S(1)}, u32[]{:S(2)}, u32[]{:S(2)}) collective-permute-start(bf16[64,2048]{1,0:T(8,128)(2,1)S(1)} %maximum_select_fusion.8), channel_id=1, source_target_pairs={{0,4},{1,5},{2,6},{3,7},{4,0},{5,1},{6,2},{7,3},{8,12},{9,13},{10,... | collective-permute-start | bytes 786440 | tf_op jit(solution)/shard_map/ppermute | solution.py:12
  26.5 13.1 %collective-permute-start.3 = (bf16[128,2048]{1,0:T(8,128)(2,1)S(1)}, bf16[128,2048]{1,0:T(8,128)(2,1)S(1)}, u32[]{:S(2)}, u32[]{:S(2)}) collective-permute-start(bf16[128,2048]{1,0:T(8,128)(2,1)S(1)} %maximum_select_fusion.7), channel_id=1, source_target_pairs={{0,8},{1,9},{2,10},{3,11},{4,12},{5,13},{6,14},{7,15},{8,0},{9,1},... | collective-permute-start | bytes 1572872 | tf_op jit(solution)/shard_map/ppermute | solution.py:12
  39.9 59.4 %copy-start.2 = (bf16[256,2048]{1,0:T(8,128)(2,1)}, bf16[256,2048]{1,0:T(8,128)(2,1)S(1)}, u32[]{:S(2)}) copy-start(bf16[256,2048]{1,0:T(8,128)(2,1)S(1)} %maximum_select_fusion.6) | copy-start | bytes 3145732
  39.9 59.4 %collective-permute-start.4 = (bf16[256,2048]{1,0:T(8,128)(2,1)S(1)}, bf16[256,2048]{1,0:T(8,128)(2,1)S(1)}, u32[]{:S(2)}, u32[]{:S(2)}) collective-permute-start(bf16[256,2048]{1,0:T(8,128)(2,1)S(1)} %maximum_select_fusion.6), channel_id=1, source_target_pairs={{0,16},{1,17},{2,18},{3,19},{4,20},{5,21},{6,22},{7,23},{8,24},{9,... | collective-permute-start | bytes 3145736 | tf_op jit(solution)/shard_map/ppermute | solution.py:12
  92.9 3.5 %copy-start.1 = (bf16[1,1024,1024]{2,1,0:T(8,128)(2,1)S(1)}, bf16[1,1024,1024]{2,1,0:T(8,128)(2,1)}, u32[]{:S(2)}) copy-start(bf16[1,1024,1024]{2,1,0:T(8,128)(2,1)} %all-gather.5.cloned.1.call-done) | copy-start | bytes 6291460
  99.3 1.0 copy-start.6
Sparse Core Ops, SparseCore 0:
  10.9 81.9 all-gather.4
  95.7 63.8 all-gather.2
